TPU v7x, 32 devices: a whole 2x2x4 slice. The times are simulated.
32 devices in a mesh: chain: 4 (over x, core), col: 8 (over z, y).
Axes of the slice: x: 2, y: 2, z: 4, core: 2. Of those that a mesh axis runs over, the one named last changes fastest.
Arguments:
- rhs: float32 [4, 8, 64, 128], P('chain', 'col'), may hold values from -6 to 6
- inverse: float32 [4, 8, 128, 128], P('chain', 'col'), as said below
- factor: float32 [4, 8, 8, 128, 128], P('chain', 'col'), may hold values from -0.1875 to 0.1875
- pattern: int32 [4, 8, 8], P('chain', 'col'), may hold values from 0 to 7, as said below
Outputs:
- forward: float32 [4, 8, 64, 128], P('chain', 'col')
- solution: float32 [4, 8, 64, 128], P('chain', 'col')
Inputs may be any that keep to these rules, and one draw needn't show every extreme that they name: `pattern`: the 8 block rows of one supernode are distinct. `inverse`: each block is lower triangular, its diagonal between 0.5 and 1.5.
All inputs are finite; a program needn't handle non-finite values.
Results may differ from a plain program's by a relative error of at most 0.00012.
Values sent between devices are 32-bit elements; how exact they have to be, the bound alone decides.
A program may use at most 64 MiB of HBM per device.

v0:
```python
import jax
import jax.numpy as jnp
from jax import lax
from jax.sharding import PartitionSpec as P


def shifted(value, axis, steps):
    count = lax.axis_size(axis)
    first, last = (max(0, -steps), min(count, count - steps))
    return lax.ppermute(value, axis, [(source, source + steps) for source in range(first, last)])


def body(rhs, inverse, factor, pattern):
    levels = lax.axis_size("chain")
    supers = lax.axis_size("col")
    highest = lax.Precision.HIGHEST
    loads_block = rhs[0, 0]
    diag_inverse = inverse[0, 0]
    blocks = factor[0, 0]
    targets = pattern[0, 0]
    loads, width = loads_block.shape
    place = lax.axis_index("chain")
    onehot = (targets[:, None] == jnp.arange(supers, dtype=jnp.int32)[None, :]).astype(jnp.float32)
    pieces = 1
    rows = loads // pieces
    steps = levels + pieces - 1

    def window(step, lag):
        index = step - lag
        live = (index >= 0) & (index < pieces)
        start = jnp.clip(index, 0, pieces - 1) * rows
        return (live, start)

    def forward_step(step, carry):
        solved, incoming = carry
        live, start = window(step, place)
        residue = loads_block - incoming
        fresh = jnp.dot(residue, diag_inverse.T, precision=highest)
        solved = jnp.where(live, fresh, solved)
        terms = jnp.einsum("rb,kab->kra", fresh, blocks, precision=highest)
        spread = jnp.einsum("kc,kra->cra", onehot, terms, precision=highest)
        received = lax.all_to_all(spread, "col", split_axis=0, concat_axis=0, tiled=True)
        summed_rows = jnp.sum(received, axis=0)
        arrived = shifted(summed_rows, "chain", 1)
        got, into = window(step + 1, place)
        got = got & (place > 0)
        incoming = jnp.where(got, arrived, incoming)
        return (solved, incoming)

    empty = jnp.zeros((loads, width), jnp.float32)
    solved, unused = lax.fori_loop(0, steps, forward_step, (empty, empty))

    def backward_step(step, carry):
        answer, outgoing = carry
        lag = levels - 1 - place
        live, start = window(step, lag)
        residue = solved - outgoing
        fresh = jnp.dot(residue, diag_inverse, precision=highest)
        answer = jnp.where(live, fresh, answer)
        arrived = shifted(fresh, "chain", -1)
        picked = jnp.einsum(
            "kc,cra->kra",
            onehot,
            lax.all_gather(arrived[None], "col", axis=0, tiled=True),
            precision=highest,
        )
        term = jnp.einsum("kra,kab->rb", picked, blocks, precision=highest)
        got, into = window(step, lag - 1)
        got = got & (place < levels - 1)
        outgoing = jnp.where(got, term, outgoing)
        return (answer, outgoing)

    answer, unused_rows = lax.fori_loop(0, steps, backward_step, (empty, empty))
    return (solved[None, None], answer[None, None])


def solution(mesh):
    in_specs = (
        P("chain", "col", None, None),
        P("chain", "col", None, None),
        P("chain", "col", None, None, None),
        P("chain", "col", None),
    )
    out_specs = (P("chain", "col", None, None), P("chain", "col", None, None))
    return jax.shard_map(body, mesh=mesh, in_specs=in_specs, out_specs=out_specs, check_vma=False)
```

profile of v0, /device:TPU:2, one launch (start us, length us, event | category | flops | bytes accessed | tf_op | source)
XLA Modules:
  0.0 230.1 jit_solution(17042671163509285255)
XLA Ops:
  1.3 82.6 %while.35 = (s32[]{:T(128)}, f32[64,128]{1,0:T(8,128)S(1)}, f32[64,128]{1,0:T(8,128)S(1)}, s32[]{:T(128)}, f32[64,128]{1,0:T(8,128)}, /*index=5*/f32[128,128]{1,...) while((s32[]{:T(128)}, f32[64,128]{1,0:T(8,128)S(1)}, ...), condition=%wide.region_2.3_spmd.clone, body=%wide.region_0.2_spmd.clone.sunk | while | flops 119644296 | bytes 3146003 | solution.py:51
  1.3 1.1 select_select_fusion.6
  2.4 1.7 fusion.53
  4.7 14.6 %all_to_all.12 = f32[8,64,128]{2,1,0:T(8,128)S(1)} all-to-all(f32[8,64,128]{2,1,0:T(8,128)S(1)} %copy.25), channel_id=1, replica_groups=mesh['chain'=4,'col'=8] {'col'}, dimensions={0} | all-to-all | bytes 524288 | tf_op jit(solution)/shard_map/while/body/eval_jaxpr/all_to_all | solution.py:42
  19.3 1.9 collective-permute-start
  21.2 3.3 %collective-permute-done = f32[64,128]{1,0:T(8,128)S(1)} collective-permute-done((f32[64,128]{1,0:T(8,128)S(1)}, f32[64,128]{1,0:T(8,128)S(1)}, u32[]{:S(2)}, u32[]{:S(2)}) %collective-permute-start) | collective-permute-done | bytes 32800 | tf_op jit(solution)/shard_map/while/body/eval_jaxpr/ppermute | solution.py:10
  24.5 1.1 select_select_fusion.6
  25.6 1.7 fusion.53
  27.9 11.6 %all_to_all.12 = f32[8,64,128]{2,1,0:T(8,128)S(1)} all-to-all(f32[8,64,128]{2,1,0:T(8,128)S(1)} %copy.25), channel_id=1, replica_groups=mesh['chain'=4,'col'=8] {'col'}, dimensions={0} | all-to-all | bytes 524288 | tf_op jit(solution)/shard_map/while/body/eval_jaxpr/all_to_all | solution.py:42
  39.5 1.9 collective-permute-start
  41.5 3.3 %collective-permute-done = f32[64,128]{1,0:T(8,128)S(1)} collective-permute-done((f32[64,128]{1,0:T(8,128)S(1)}, f32[64,128]{1,0:T(8,128)S(1)}, u32[]{:S(2)}, u32[]{:S(2)}) %collective-permute-start) | collective-permute-done | bytes 32800 | tf_op jit(solution)/shard_map/while/body/eval_jaxpr/ppermute | solution.py:10
  45.9 1.7 fusion.53
  48.2 10.9 %all_to_all.12 = f32[8,64,128]{2,1,0:T(8,128)S(1)} all-to-all(f32[8,64,128]{2,1,0:T(8,128)S(1)} %copy.25), channel_id=1, replica_groups=mesh['chain'=4,'col'=8] {'col'}, dimensions={0} | all-to-all | bytes 524288 | tf_op jit(solution)/shard_map/while/body/eval_jaxpr/all_to_all | solution.py:42
  59.1 1.9 collective-permute-start
  61.0 3.3 %collective-permute-done = f32[64,128]{1,0:T(8,128)S(1)} collective-permute-done((f32[64,128]{1,0:T(8,128)S(1)}, f32[64,128]{1,0:T(8,128)S(1)}, u32[]{:S(2)}, u32[]{:S(2)}) %collective-permute-start) | collective-permute-done | bytes 32800 | tf_op jit(solution)/shard_map/while/body/eval_jaxpr/ppermute | solution.py:10
  65.4 1.7 fusion.53
  67.7 10.9 %all_to_all.12 = f32[8,64,128]{2,1,0:T(8,128)S(1)} all-to-all(f32[8,64,128]{2,1,0:T(8,128)S(1)} %copy.25), channel_id=1, replica_groups=mesh['chain'=4,'col'=8] {'col'}, dimensions={0} | all-to-all | bytes 524288 | tf_op jit(solution)/shard_map/while/body/eval_jaxpr/all_to_all | solution.py:42
  78.7 1.9 collective-permute-start
  80.6 3.3 %collective-permute-done = f32[64,128]{1,0:T(8,128)S(1)} collective-permute-done((f32[64,128]{1,0:T(8,128)S(1)}, f32[64,128]{1,0:T(8,128)S(1)}, u32[]{:S(2)}, u32[]{:S(2)}) %collective-permute-start) | collective-permute-done | bytes 32800 | tf_op jit(solution)/shard_map/while/body/eval_jaxpr/ppermute | solution.py:10
  83.9 145.5 %while.36 = (s32[]{:T(128)}, f32[64,128]{1,0:T(8,128)S(1)}, f32[64,128]{1,0:T(8,128)S(1)}, s32[]{:T(128)}, f32[64,128]{1,0:T(8,128)S(1)}, /*index=5*/f32[128,128...) while((s32[]{:T(128)}, f32[64,128]{1,0:T(8,128)S(1)}, ...), condition=%wide.region_4.5_spmd.clone, body=%wide.region_3.4_spmd.clone.sunk | while | flops 119586952 | bytes 4129067 | solution.py:73
  85.1 1.9 collective-permute-start.1
  87.0 1.6 collective-permute-done.1
  88.6 30.7 %all-gather.3 = f32[512,128]{1,0:T(8,128)S(1)} all-gather(f32[64,128]{1,0:T(8,128)S(1)} %collective-permute-done.1), channel_id=2, replica_groups=mesh['chain'=4,'col'=8] {'col'}, dimensions={0}, use_global_device_ids=true | all-gather | bytes 294912 | tf_op jit(solution)/shard_map/while/body/eval_jaxpr/all_gather | solution.py:64
  121.4 1.9 collective-permute-start.1
  123.4 1.6 collective-permute-done.1
  124.9 30.7 %all-gather.3 = f32[512,128]{1,0:T(8,128)S(1)} all-gather(f32[64,128]{1,0:T(8,128)S(1)} %collective-permute-done.1), channel_id=2, replica_groups=mesh['chain'=4,'col'=8] {'col'}, dimensions={0}, use_global_device_ids=true | all-gather | bytes 294912 | tf_op jit(solution)/shard_map/while/body/eval_jaxpr/all_gather | solution.py:64
  157.8 1.9 collective-permute-start.1
  159.8 1.6 collective-permute-done.1
  161.3 30.7 %all-gather.3 = f32[512,128]{1,0:T(8,128)S(1)} all-gather(f32[64,128]{1,0:T(8,128)S(1)} %collective-permute-done.1), channel_id=2, replica_groups=mesh['chain'=4,'col'=8] {'col'}, dimensions={0}, use_global_device_ids=true | all-gather | bytes 294912 | tf_op jit(solution)/shard_map/while/body/eval_jaxpr/all_gather | solution.py:64
  194.2 1.9 collective-permute-start.1
  196.1 1.6 collective-permute-done.1
  197.7 30.7 %all-gather.3 = f32[512,128]{1,0:T(8,128)S(1)} all-gather(f32[64,128]{1,0:T(8,128)S(1)} %collective-permute-done.1), channel_id=2, replica_groups=mesh['chain'=4,'col'=8] {'col'}, dimensions={0}, use_global_device_ids=true | all-gather | bytes 294912 | tf_op jit(solution)/shard_map/while/body/eval_jaxpr/all_gather | solution.py:64
  (48 shorter events, 14.1 us)
Async XLA Ops:
  0.7 0.7 copy-start.3
  19.3 5.2 %collective-permute-start = (f32[64,128]{1,0:T(8,128)S(1)}, f32[64,128]{1,0:T(8,128)S(1)}, u32[]{:S(2)}, u32[]{:S(2)}) collective-permute-start(f32[64,128]{1,0:T(8,128)S(1)} %reduce_sum.16), channel_id=1, source_target_pairs={{0,8},{8,16},{16,24},{1,9},{9,17},{17,25},{2,10},{10,18},{18,26},{... | collective-permute-start | bytes 98312 | tf_op jit(solution)/shard_map/while/body/eval_jaxpr/ppermute | solution.py:10
  39.5 5.2 %collective-permute-start = (f32[64,128]{1,0:T(8,128)S(1)}, f32[64,128]{1,0:T(8,128)S(1)}, u32[]{:S(2)}, u32[]{:S(2)}) collective-permute-start(f32[64,128]{1,0:T(8,128)S(1)} %reduce_sum.16), channel_id=1, source_target_pairs={{0,8},{8,16},{16,24},{1,9},{9,17},{17,25},{2,10},{10,18},{18,26},{... | collective-permute-start | bytes 98312 | tf_op jit(solution)/shard_map/while/body/eval_jaxpr/ppermute | solution.py:10
  59.1 5.2 %collective-permute-start = (f32[64,128]{1,0:T(8,128)S(1)}, f32[64,128]{1,0:T(8,128)S(1)}, u32[]{:S(2)}, u32[]{:S(2)}) collective-permute-start(f32[64,128]{1,0:T(8,128)S(1)} %reduce_sum.16), channel_id=1, source_target_pairs={{0,8},{8,16},{16,24},{1,9},{9,17},{17,25},{2,10},{10,18},{18,26},{... | collective-permute-start | bytes 98312 | tf_op jit(solution)/shard_map/while/body/eval_jaxpr/ppermute | solution.py:10
  78.7 5.2 %collective-permute-start = (f32[64,128]{1,0:T(8,128)S(1)}, f32[64,128]{1,0:T(8,128)S(1)}, u32[]{:S(2)}, u32[]{:S(2)}) collective-permute-start(f32[64,128]{1,0:T(8,128)S(1)} %reduce_sum.16), channel_id=1, source_target_pairs={{0,8},{8,16},{16,24},{1,9},{9,17},{17,25},{2,10},{10,18},{18,26},{... | collective-permute-start | bytes 98312 | tf_op jit(solution)/shard_map/while/body/eval_jaxpr/ppermute | solution.py:10
  84.0 35.9 %copy-start = (f32[8,128,128]{2,1,0:T(8,128)S(1)}, f32[8,128,128]{2,1,0:T(8,128)}, u32[]{:S(2)}) copy-start(f32[8,128,128]{2,1,0:T(8,128)} %get-tuple-element.685) | copy-start | bytes 1572868 | tf_op jit(solution)/shard_map/while
  85.1 3.5 %collective-permute-start.1 = (f32[64,128]{1,0:T(8,128)S(1)}, f32[64,128]{1,0:T(8,128)S(1)}, u32[]{:S(2)}, u32[]{:S(2)}) collective-permute-start(f32[64,128]{1,0:T(8,128)S(1)} %get-tuple-element.616), channel_id=1, source_target_pairs={{8,0},{16,8},{24,16},{9,1},{17,9},{25,17},{10,2},{18,10},{26,18},{... | collective-permute-start | bytes 98312 | tf_op jit(solution)/shard_map/while/body/eval_jaxpr/ppermute | solution.py:10
  120.3 35.9 %copy-start = (f32[8,128,128]{2,1,0:T(8,128)S(1)}, f32[8,128,128]{2,1,0:T(8,128)}, u32[]{:S(2)}) copy-start(f32[8,128,128]{2,1,0:T(8,128)} %get-tuple-element.685) | copy-start | bytes 1572868 | tf_op jit(solution)/shard_map/while
  121.4 3.5 %collective-permute-start.1 = (f32[64,128]{1,0:T(8,128)S(1)}, f32[64,128]{1,0:T(8,128)S(1)}, u32[]{:S(2)}, u32[]{:S(2)}) collective-permute-start(f32[64,128]{1,0:T(8,128)S(1)} %get-tuple-element.616), channel_id=1, source_target_pairs={{8,0},{16,8},{24,16},{9,1},{17,9},{25,17},{10,2},{18,10},{26,18},{... | collective-permute-start | bytes 98312 | tf_op jit(solution)/shard_map/while/body/eval_jaxpr/ppermute | solution.py:10
  156.7 35.9 %copy-start = (f32[8,128,128]{2,1,0:T(8,128)S(1)}, f32[8,128,128]{2,1,0:T(8,128)}, u32[]{:S(2)}) copy-start(f32[8,128,128]{2,1,0:T(8,128)} %get-tuple-element.685) | copy-start | bytes 1572868 | tf_op jit(solution)/shard_map/while
  157.8 3.5 %collective-permute-start.1 = (f32[64,128]{1,0:T(8,128)S(1)}, f32[64,128]{1,0:T(8,128)S(1)}, u32[]{:S(2)}, u32[]{:S(2)}) collective-permute-start(f32[64,128]{1,0:T(8,128)S(1)} %get-tuple-element.616), channel_id=1, source_target_pairs={{8,0},{16,8},{24,16},{9,1},{17,9},{25,17},{10,2},{18,10},{26,18},{... | collective-permute-start | bytes 98312 | tf_op jit(solution)/shard_map/while/body/eval_jaxpr/ppermute | solution.py:10
  193.1 35.9 %copy-start = (f32[8,128,128]{2,1,0:T(8,128)S(1)}, f32[8,128,128]{2,1,0:T(8,128)}, u32[]{:S(2)}) copy-start(f32[8,128,128]{2,1,0:T(8,128)} %get-tuple-element.685) | copy-start | bytes 1572868 | tf_op jit(solution)/shard_map/while
  194.2 3.5 %collective-permute-start.1 = (f32[64,128]{1,0:T(8,128)S(1)}, f32[64,128]{1,0:T(8,128)S(1)}, u32[]{:S(2)}, u32[]{:S(2)}) collective-permute-start(f32[64,128]{1,0:T(8,128)S(1)} %get-tuple-element.616), channel_id=1, source_target_pairs={{8,0},{16,8},{24,16},{9,1},{17,9},{25,17},{10,2},{18,10},{26,18},{... | collective-permute-start | bytes 98312 | tf_op jit(solution)/shard_map/while/body/eval_jaxpr/ppermute | solution.py:10
  229.4 0.6 copy-start.1
  229.5 0.6 copy-start.2
where the time goes:
time: 231 us; the launch traced here: 230 us
  blocking collectives  171 us (74%)
  matrix products  21.5 us (9%)
  waiting for transfers between devices  19.4 us (8%)
  starting transfers between devices  15.4 us (7%)
    all_gather x4, blocking collectives, backward_step(): lax.all_gather(arrived[None], 'col', axis=0, tiled=True)  123 us
    all_to_all x4, blocking collectives, forward_step(): lax.all_to_all(spread, 'col', split_axis=0, concat_axis=0, tiled=True)  48 us
    ppermute x8, waiting for transfers between devices, shifted(): lax.ppermute(value, axis, [(source, source + steps) for source in range(f...  19.4 us
    ppermute x8, starting transfers between devices, shifted(): lax.ppermute(value, axis, [(source, source + steps) for source in range(f...  15.4 us
    dot_general x4, matrix products, forward_step(): terms = jnp.einsum('rb,kab->kra', fresh, blocks, precision=highest)  6.82 us
  transfers between devices with their start and end apart: 8, of which 8 were waited for; matrix products, arithmetic and copies ran while one was open for 0% of the time, Pallas kernels for 0%

commit v1 on v0

--- a/solution.py
+++ b/solution.py
@@ -58,12 +58,42 @@
         fresh = jnp.dot(residue, diag_inverse, precision=highest)
         answer = jnp.where(live, fresh, answer)
         arrived = shifted(fresh, "chain", -1)
-        picked = jnp.einsum(
+        peers, index_2, rows_2 = (
+            lax.axis_size("col"),
+            lax.axis_index("col"),
+            arrived[None].shape[0],
+        )
+        right = [(i, (i + 1) % peers) for i in range(peers)]
+        left = [(i, (i - 1) % peers) for i in range(peers)]
+        half = peers // 2
+        from_left = from_right = arrived[None]
+        running = jnp.einsum(
             "kc,cra->kra",
-            onehot,
-            lax.all_gather(arrived[None], "col", axis=0, tiled=True),
+            lax.dynamic_slice_in_dim(onehot, index_2 * rows_2, arrived[None].shape[0], axis=1),
+            arrived[None],
             precision=highest,
         )
+        for turn in range(1, half + 1):
+            from_left = lax.ppermute(from_left, "col", right)
+            if turn < peers - half:
+                from_right = lax.ppermute(from_right, "col", left)
+                running = running + jnp.einsum(
+                    "kc,cra->kra",
+                    lax.dynamic_slice_in_dim(
+                        onehot, (index_2 + turn) % peers * rows_2, from_right.shape[0], axis=1
+                    ),
+                    from_right,
+                    precision=highest,
+                )
+            running = running + jnp.einsum(
+                "kc,cra->kra",
+                lax.dynamic_slice_in_dim(
+                    onehot, (index_2 - turn) % peers * rows_2, from_left.shape[0], axis=1
+                ),
+                from_left,
+                precision=highest,
+            )
+        picked = running
         term = jnp.einsum("kra,kab->rb", picked, blocks, precision=highest)
         got, into = window(step, lag - 1)
         got = got & (place < levels - 1)

time: 231 us -> 212 us (0.918)
  blocking collectives: 171 us -> 48 us
  starting transfers between devices: 15.4 us -> 72.1 us
  waiting for transfers between devices: 19.4 us -> 68.4 us
    all_gather x4 -> x0, blocking collectives: 123 us -> none  [backward_step(): lax.all_gather(arrived[None], 'col', axis=0, tiled=True)]
    ppermute x0 -> x28, starting transfers between devices: none -> 56.7 us  [the longest x12 56.6 us: backward_step(): from_right = lax.ppermute(from_right, 'col', left)]
    ppermute x0 -> x28, waiting for transfers between devices: none -> 48.9 us  [the longest x16 48.9 us: backward_step(): from_left = lax.ppermute(from_left, 'col', right)]
  transfers between devices with their start and end apart: 8 -> 36, of which waited for: 8 -> 24; matrix products, arithmetic and copies ran while one was open for 0% -> 0% of each run, Pallas kernels for 0% -> 0%
where the time goes in v1:
time: 212 us; the launch traced here: 211 us
  starting transfers between devices  72.1 us (34%)
  waiting for transfers between devices  68.4 us (32%)
  blocking collectives  48 us (23%)
  matrix products  20.1 us (9%)
    ppermute x12, starting transfers between devices, backward_step(): from_right = lax.ppermute(from_right, 'col', left)  56.6 us
    ppermute x16, waiting for transfers between devices, backward_step(): from_left = lax.ppermute(from_left, 'col', right)  48.9 us
    all_to_all x4, blocking collectives, forward_step(): lax.all_to_all(spread, 'col', split_axis=0, concat_axis=0, tiled=True)  48 us
    ppermute x8, waiting for transfers between devices, shifted(): lax.ppermute(value, axis, [(source, source + steps) for source in range(f...  19.5 us
    ppermute x8, starting transfers between devices, shifted(): lax.ppermute(value, axis, [(source, source + steps) for source in range(f...  15.4 us
    dot_general x4, matrix products, forward_step(): terms = jnp.einsum('rb,kab->kra', fresh, blocks, precision=highest)  6.82 us
    dot_general x4, matrix products, forward_step(): fresh = jnp.dot(residue, diag_inverse.T, precision=highest)  4.4 us
    dot_general x4, matrix products, backward_step(): fresh = jnp.dot(residue, diag_inverse, precision=highest)  4.32 us
  transfers between devices with their start and end apart: 36, of which 24 were waited for; matrix products, arithmetic and copies ran while one was open for 0% of the time, Pallas kernels for 0%

profile of v1, /device:TPU:2, one launch (start us, length us, event | category | flops | bytes accessed | tf_op | source)
XLA Modules:
  0.0 211.5 jit_solution(7619192039612939305)
XLA Ops:
  1.3 82.6 %while.36 = (s32[]{:T(128)}, f32[64,128]{1,0:T(8,128)S(1)}, f32[64,128]{1,0:T(8,128)S(1)}, s32[]{:T(128)}, f32[64,128]{1,0:T(8,128)}, /*index=5*/f32[128,128]{1,...) while((s32[]{:T(128)}, f32[64,128]{1,0:T(8,128)S(1)}, ...), condition=%wide.region_2.3_spmd.clone, body=%wide.region_0.2_spmd.clone.sunk | while | flops 119644296 | bytes 3146003 | solution.py:51
  4.7 14.6 %all_to_all.12 = f32[8,64,128]{2,1,0:T(8,128)S(1)} all-to-all(f32[8,64,128]{2,1,0:T(8,128)S(1)} %copy.15), channel_id=1, replica_groups=mesh['chain'=4,'col'=8] {'col'}, dimensions={0} | all-to-all | bytes 524288 | tf_op jit(solution)/shard_map/while/body/eval_jaxpr/all_to_all | solution.py:42
  19.3 1.9 collective-permute-start
  21.2 3.3 %collective-permute-done = f32[64,128]{1,0:T(8,128)S(1)} collective-permute-done((f32[64,128]{1,0:T(8,128)S(1)}, f32[64,128]{1,0:T(8,128)S(1)}, u32[]{:S(2)}, u32[]{:S(2)}) %collective-permute-start) | collective-permute-done | bytes 32800 | tf_op jit(solution)/shard_map/while/body/eval_jaxpr/ppermute | solution.py:10
  27.9 11.6 %all_to_all.12 = f32[8,64,128]{2,1,0:T(8,128)S(1)} all-to-all(f32[8,64,128]{2,1,0:T(8,128)S(1)} %copy.15), channel_id=1, replica_groups=mesh['chain'=4,'col'=8] {'col'}, dimensions={0} | all-to-all | bytes 524288 | tf_op jit(solution)/shard_map/while/body/eval_jaxpr/all_to_all | solution.py:42
  39.5 1.9 collective-permute-start
  41.5 3.3 %collective-permute-done = f32[64,128]{1,0:T(8,128)S(1)} collective-permute-done((f32[64,128]{1,0:T(8,128)S(1)}, f32[64,128]{1,0:T(8,128)S(1)}, u32[]{:S(2)}, u32[]{:S(2)}) %collective-permute-start) | collective-permute-done | bytes 32800 | tf_op jit(solution)/shard_map/while/body/eval_jaxpr/ppermute | solution.py:10
  48.2 10.9 %all_to_all.12 = f32[8,64,128]{2,1,0:T(8,128)S(1)} all-to-all(f32[8,64,128]{2,1,0:T(8,128)S(1)} %copy.15), channel_id=1, replica_groups=mesh['chain'=4,'col'=8] {'col'}, dimensions={0} | all-to-all | bytes 524288 | tf_op jit(solution)/shard_map/while/body/eval_jaxpr/all_to_all | solution.py:42
  59.1 1.9 collective-permute-start
  61.0 3.3 %collective-permute-done = f32[64,128]{1,0:T(8,128)S(1)} collective-permute-done((f32[64,128]{1,0:T(8,128)S(1)}, f32[64,128]{1,0:T(8,128)S(1)}, u32[]{:S(2)}, u32[]{:S(2)}) %collective-permute-start) | collective-permute-done | bytes 32800 | tf_op jit(solution)/shard_map/while/body/eval_jaxpr/ppermute | solution.py:10
  67.7 10.9 %all_to_all.12 = f32[8,64,128]{2,1,0:T(8,128)S(1)} all-to-all(f32[8,64,128]{2,1,0:T(8,128)S(1)} %copy.15), channel_id=1, replica_groups=mesh['chain'=4,'col'=8] {'col'}, dimensions={0} | all-to-all | bytes 524288 | tf_op jit(solution)/shard_map/while/body/eval_jaxpr/all_to_all | solution.py:42
  78.7 1.9 collective-permute-start
  80.6 3.3 %collective-permute-done = f32[64,128]{1,0:T(8,128)S(1)} collective-permute-done((f32[64,128]{1,0:T(8,128)S(1)}, f32[64,128]{1,0:T(8,128)S(1)}, u32[]{:S(2)}, u32[]{:S(2)}) %collective-permute-start) | collective-permute-done | bytes 32800 | tf_op jit(solution)/shard_map/while/body/eval_jaxpr/ppermute | solution.py:10
  83.9 126.9 %while.37 = (s32[]{:T(128)}, f32[64,128]{1,0:T(8,128)S(1)}, f32[64,128]{1,0:T(8,128)S(1)}, s32[]{:T(128)}, f32[64,128]{1,0:T(8,128)S(1)}, /*index=5*/f32[128,128...) while((s32[]{:T(128)}, f32[64,128]{1,0:T(8,128)S(1)}, ...), condition=%wide.region_4.5_spmd.clone, body=%wide.region_3.4_spmd.clone.sunk | while | flops 114278520 | bytes 4229630 | solution.py:103
  88.6 4.7 %collective-permute-start.6 = (f32[1,64,128]{2,1,0:T(8,128)S(1)}, f32[1,64,128]{2,1,0:T(8,128)S(1)}, u32[]{:S(2)}, u32[]{:S(2)}) collective-permute-start(f32[1,64,128]{2,1,0:T(8,128)S(1)} %bitcast.92), channel_id=1, source_target_pairs={{0,7},{1,0},{2,1},{3,2},{4,3},{5,4},{6,5},{7,6},{8,15},{9,8},{10,9... | collective-permute-start | bytes 98312 | tf_op jit(solution)/shard_map/while/body/eval_jaxpr/ppermute | solution.py:79
  95.2 4.7 %collective-permute-start.7 = (f32[1,64,128]{2,1,0:T(8,128)S(1)}, f32[1,64,128]{2,1,0:T(8,128)S(1)}, u32[]{:S(2)}, u32[]{:S(2)}) collective-permute-start(f32[1,64,128]{2,1,0:T(8,128)S(1)} %collective-permute-done.6), channel_id=1, source_target_pairs={{0,7},{1,0},{2,1},{3,2},{4,3},{5,4},{6,5},{7,6},{8,15},{9,8},{10,9... | collective-permute-start | bytes 98312 | tf_op jit(solution)/shard_map/while/body/eval_jaxpr/ppermute | solution.py:79
  101.8 4.7 %collective-permute-start.8 = (f32[1,64,128]{2,1,0:T(8,128)S(1)}, f32[1,64,128]{2,1,0:T(8,128)S(1)}, u32[]{:S(2)}, u32[]{:S(2)}) collective-permute-start(f32[1,64,128]{2,1,0:T(8,128)S(1)} %collective-permute-done.7), channel_id=1, source_target_pairs={{0,7},{1,0},{2,1},{3,2},{4,3},{5,4},{6,5},{7,6},{8,15},{9,8},{10,9... | collective-permute-start | bytes 98312 | tf_op jit(solution)/shard_map/while/body/eval_jaxpr/ppermute | solution.py:79
  108.5 6.6 %collective-permute-done.5 = f32[1,64,128]{2,1,0:T(8,128)S(1)} collective-permute-done((f32[1,64,128]{2,1,0:T(8,128)S(1)}, f32[1,64,128]{2,1,0:T(8,128)S(1)}, u32[]{:S(2)}, u32[]{:S(2)}) %collective-permute-start.5) | collective-permute-done | bytes 32800 | tf_op jit(solution)/shard_map/while/body/eval_jaxpr/ppermute | solution.py:77
  120.3 4.7 %collective-permute-start.6 = (f32[1,64,128]{2,1,0:T(8,128)S(1)}, f32[1,64,128]{2,1,0:T(8,128)S(1)}, u32[]{:S(2)}, u32[]{:S(2)}) collective-permute-start(f32[1,64,128]{2,1,0:T(8,128)S(1)} %bitcast.92), channel_id=1, source_target_pairs={{0,7},{1,0},{2,1},{3,2},{4,3},{5,4},{6,5},{7,6},{8,15},{9,8},{10,9... | collective-permute-start | bytes 98312 | tf_op jit(solution)/shard_map/while/body/eval_jaxpr/ppermute | solution.py:79
  126.9 4.7 %collective-permute-start.7 = (f32[1,64,128]{2,1,0:T(8,128)S(1)}, f32[1,64,128]{2,1,0:T(8,128)S(1)}, u32[]{:S(2)}, u32[]{:S(2)}) collective-permute-start(f32[1,64,128]{2,1,0:T(8,128)S(1)} %collective-permute-done.6), channel_id=1, source_target_pairs={{0,7},{1,0},{2,1},{3,2},{4,3},{5,4},{6,5},{7,6},{8,15},{9,8},{10,9... | collective-permute-start | bytes 98312 | tf_op jit(solution)/shard_map/while/body/eval_jaxpr/ppermute | solution.py:79
  133.5 4.7 %collective-permute-start.8 = (f32[1,64,128]{2,1,0:T(8,128)S(1)}, f32[1,64,128]{2,1,0:T(8,128)S(1)}, u32[]{:S(2)}, u32[]{:S(2)}) collective-permute-start(f32[1,64,128]{2,1,0:T(8,128)S(1)} %collective-permute-done.7), channel_id=1, source_target_pairs={{0,7},{1,0},{2,1},{3,2},{4,3},{5,4},{6,5},{7,6},{8,15},{9,8},{10,9... | collective-permute-start | bytes 98312 | tf_op jit(solution)/shard_map/while/body/eval_jaxpr/ppermute | solution.py:79
  140.2 6.6 %collective-permute-done.5 = f32[1,64,128]{2,1,0:T(8,128)S(1)} collective-permute-done((f32[1,64,128]{2,1,0:T(8,128)S(1)}, f32[1,64,128]{2,1,0:T(8,128)S(1)}, u32[]{:S(2)}, u32[]{:S(2)}) %collective-permute-start.5) | collective-permute-done | bytes 32800 | tf_op jit(solution)/shard_map/while/body/eval_jaxpr/ppermute | solution.py:77
  148.5 1.9 collective-permute-start.1
  152.0 4.7 %collective-permute-start.6 = (f32[1,64,128]{2,1,0:T(8,128)S(1)}, f32[1,64,128]{2,1,0:T(8,128)S(1)}, u32[]{:S(2)}, u32[]{:S(2)}) collective-permute-start(f32[1,64,128]{2,1,0:T(8,128)S(1)} %bitcast.92), channel_id=1, source_target_pairs={{0,7},{1,0},{2,1},{3,2},{4,3},{5,4},{6,5},{7,6},{8,15},{9,8},{10,9... | collective-permute-start | bytes 98312 | tf_op jit(solution)/shard_map/while/body/eval_jaxpr/ppermute | solution.py:79
  158.6 4.7 %collective-permute-start.7 = (f32[1,64,128]{2,1,0:T(8,128)S(1)}, f32[1,64,128]{2,1,0:T(8,128)S(1)}, u32[]{:S(2)}, u32[]{:S(2)}) collective-permute-start(f32[1,64,128]{2,1,0:T(8,128)S(1)} %collective-permute-done.6), channel_id=1, source_target_pairs={{0,7},{1,0},{2,1},{3,2},{4,3},{5,4},{6,5},{7,6},{8,15},{9,8},{10,9... | collective-permute-start | bytes 98312 | tf_op jit(solution)/shard_map/while/body/eval_jaxpr/ppermute | solution.py:79
  165.3 4.7 %collective-permute-start.8 = (f32[1,64,128]{2,1,0:T(8,128)S(1)}, f32[1,64,128]{2,1,0:T(8,128)S(1)}, u32[]{:S(2)}, u32[]{:S(2)}) collective-permute-start(f32[1,64,128]{2,1,0:T(8,128)S(1)} %collective-permute-done.7), channel_id=1, source_target_pairs={{0,7},{1,0},{2,1},{3,2},{4,3},{5,4},{6,5},{7,6},{8,15},{9,8},{10,9... | collective-permute-start | bytes 98312 | tf_op jit(solution)/shard_map/while/body/eval_jaxpr/ppermute | solution.py:79
  171.9 6.6 %collective-permute-done.5 = f32[1,64,128]{2,1,0:T(8,128)S(1)} collective-permute-done((f32[1,64,128]{2,1,0:T(8,128)S(1)}, f32[1,64,128]{2,1,0:T(8,128)S(1)}, u32[]{:S(2)}, u32[]{:S(2)}) %collective-permute-start.5) | collective-permute-done | bytes 32800 | tf_op jit(solution)/shard_map/while/body/eval_jaxpr/ppermute | solution.py:77
  180.2 1.9 collective-permute-start.1
  183.8 4.7 %collective-permute-start.6 = (f32[1,64,128]{2,1,0:T(8,128)S(1)}, f32[1,64,128]{2,1,0:T(8,128)S(1)}, u32[]{:S(2)}, u32[]{:S(2)}) collective-permute-start(f32[1,64,128]{2,1,0:T(8,128)S(1)} %bitcast.92), channel_id=1, source_target_pairs={{0,7},{1,0},{2,1},{3,2},{4,3},{5,4},{6,5},{7,6},{8,15},{9,8},{10,9... | collective-permute-start | bytes 98312 | tf_op jit(solution)/shard_map/while/body/eval_jaxpr/ppermute | solution.py:79
  190.4 4.7 %collective-permute-start.7 = (f32[1,64,128]{2,1,0:T(8,128)S(1)}, f32[1,64,128]{2,1,0:T(8,128)S(1)}, u32[]{:S(2)}, u32[]{:S(2)}) collective-permute-start(f32[1,64,128]{2,1,0:T(8,128)S(1)} %collective-permute-done.6), channel_id=1, source_target_pairs={{0,7},{1,0},{2,1},{3,2},{4,3},{5,4},{6,5},{7,6},{8,15},{9,8},{10,9... | collective-permute-start | bytes 98312 | tf_op jit(solution)/shard_map/while/body/eval_jaxpr/ppermute | solution.py:79
  197.0 4.7 %collective-permute-start.8 = (f32[1,64,128]{2,1,0:T(8,128)S(1)}, f32[1,64,128]{2,1,0:T(8,128)S(1)}, u32[]{:S(2)}, u32[]{:S(2)}) collective-permute-start(f32[1,64,128]{2,1,0:T(8,128)S(1)} %collective-permute-done.7), channel_id=1, source_target_pairs={{0,7},{1,0},{2,1},{3,2},{4,3},{5,4},{6,5},{7,6},{8,15},{9,8},{10,9... | collective-permute-start | bytes 98312 | tf_op jit(solution)/shard_map/while/body/eval_jaxpr/ppermute | solution.py:79
  203.6 6.6 %collective-permute-done.5 = f32[1,64,128]{2,1,0:T(8,128)S(1)} collective-permute-done((f32[1,64,128]{2,1,0:T(8,128)S(1)}, f32[1,64,128]{2,1,0:T(8,128)S(1)}, u32[]{:S(2)}, u32[]{:S(2)}) %collective-permute-start.5) | collective-permute-done | bytes 32800 | tf_op jit(solution)/shard_map/while/body/eval_jaxpr/ppermute | solution.py:77
  (101 shorter events, 54.6 us)
Async XLA Ops:
  19.3 5.2 %collective-permute-start = (f32[64,128]{1,0:T(8,128)S(1)}, f32[64,128]{1,0:T(8,128)S(1)}, u32[]{:S(2)}, u32[]{:S(2)}) collective-permute-start(f32[64,128]{1,0:T(8,128)S(1)} %reduce_sum.16), channel_id=1, source_target_pairs={{0,8},{8,16},{16,24},{1,9},{9,17},{17,25},{2,10},{10,18},{18,26},{... | collective-permute-start | bytes 98312 | tf_op jit(solution)/shard_map/while/body/eval_jaxpr/ppermute | solution.py:10
  39.5 5.2 %collective-permute-start = (f32[64,128]{1,0:T(8,128)S(1)}, f32[64,128]{1,0:T(8,128)S(1)}, u32[]{:S(2)}, u32[]{:S(2)}) collective-permute-start(f32[64,128]{1,0:T(8,128)S(1)} %reduce_sum.16), channel_id=1, source_target_pairs={{0,8},{8,16},{16,24},{1,9},{9,17},{17,25},{2,10},{10,18},{18,26},{... | collective-permute-start | bytes 98312 | tf_op jit(solution)/shard_map/while/body/eval_jaxpr/ppermute | solution.py:10
  59.1 5.2 %collective-permute-start = (f32[64,128]{1,0:T(8,128)S(1)}, f32[64,128]{1,0:T(8,128)S(1)}, u32[]{:S(2)}, u32[]{:S(2)}) collective-permute-start(f32[64,128]{1,0:T(8,128)S(1)} %reduce_sum.16), channel_id=1, source_target_pairs={{0,8},{8,16},{16,24},{1,9},{9,17},{17,25},{2,10},{10,18},{18,26},{... | collective-permute-start | bytes 98312 | tf_op jit(solution)/shard_map/while/body/eval_jaxpr/ppermute | solution.py:10
  78.7 5.2 %collective-permute-start = (f32[64,128]{1,0:T(8,128)S(1)}, f32[64,128]{1,0:T(8,128)S(1)}, u32[]{:S(2)}, u32[]{:S(2)}) collective-permute-start(f32[64,128]{1,0:T(8,128)S(1)} %reduce_sum.16), channel_id=1, source_target_pairs={{0,8},{8,16},{16,24},{1,9},{9,17},{17,25},{2,10},{10,18},{18,26},{... | collective-permute-start | bytes 98312 | tf_op jit(solution)/shard_map/while/body/eval_jaxpr/ppermute | solution.py:10
  88.6 6.6 %collective-permute-start.2 = (f32[1,64,128]{2,1,0:T(8,128)S(1)}, f32[1,64,128]{2,1,0:T(8,128)S(1)}, u32[]{:S(2)}, u32[]{:S(2)}) collective-permute-start(f32[1,64,128]{2,1,0:T(8,128)S(1)} %bitcast.91), channel_id=1, source_target_pairs={{0,1},{1,2},{2,3},{3,4},{4,5},{5,6},{6,7},{7,0},{8,9},{9,10},{10,1... | collective-permute-start | bytes 98312 | tf_op jit(solution)/shard_map/while/body/eval_jaxpr/ppermute | solution.py:77
  88.6 6.6 %collective-permute-start.6 = (f32[1,64,128]{2,1,0:T(8,128)S(1)}, f32[1,64,128]{2,1,0:T(8,128)S(1)}, u32[]{:S(2)}, u32[]{:S(2)}) collective-permute-start(f32[1,64,128]{2,1,0:T(8,128)S(1)} %bitcast.92), channel_id=1, source_target_pairs={{0,7},{1,0},{2,1},{3,2},{4,3},{5,4},{6,5},{7,6},{8,15},{9,8},{10,9... | collective-permute-start | bytes 98312 | tf_op jit(solution)/shard_map/while/body/eval_jaxpr/ppermute | solution.py:79
  95.2 6.6 %collective-permute-start.3 = (f32[1,64,128]{2,1,0:T(8,128)S(1)}, f32[1,64,128]{2,1,0:T(8,128)S(1)}, u32[]{:S(2)}, u32[]{:S(2)}) collective-permute-start(f32[1,64,128]{2,1,0:T(8,128)S(1)} %collective-permute-done.2), channel_id=1, source_target_pairs={{0,1},{1,2},{2,3},{3,4},{4,5},{5,6},{6,7},{7,0},{8,9},{9,10},{10,1... | collective-permute-start | bytes 98312 | tf_op jit(solution)/shard_map/while/body/eval_jaxpr/ppermute | solution.py:77
  95.2 6.6 %collective-permute-start.7 = (f32[1,64,128]{2,1,0:T(8,128)S(1)}, f32[1,64,128]{2,1,0:T(8,128)S(1)}, u32[]{:S(2)}, u32[]{:S(2)}) collective-permute-start(f32[1,64,128]{2,1,0:T(8,128)S(1)} %collective-permute-done.6), channel_id=1, source_target_pairs={{0,7},{1,0},{2,1},{3,2},{4,3},{5,4},{6,5},{7,6},{8,15},{9,8},{10,9... | collective-permute-start | bytes 98312 | tf_op jit(solution)/shard_map/while/body/eval_jaxpr/ppermute | solution.py:79
  101.8 6.6 %collective-permute-start.4 = (f32[1,64,128]{2,1,0:T(8,128)S(1)}, f32[1,64,128]{2,1,0:T(8,128)S(1)}, u32[]{:S(2)}, u32[]{:S(2)}) collective-permute-start(f32[1,64,128]{2,1,0:T(8,128)S(1)} %collective-permute-done.3), channel_id=1, source_target_pairs={{0,1},{1,2},{2,3},{3,4},{4,5},{5,6},{6,7},{7,0},{8,9},{9,10},{10,1... | collective-permute-start | bytes 98312 | tf_op jit(solution)/shard_map/while/body/eval_jaxpr/ppermute | solution.py:77
  101.8 6.6 %collective-permute-start.8 = (f32[1,64,128]{2,1,0:T(8,128)S(1)}, f32[1,64,128]{2,1,0:T(8,128)S(1)}, u32[]{:S(2)}, u32[]{:S(2)}) collective-permute-start(f32[1,64,128]{2,1,0:T(8,128)S(1)} %collective-permute-done.7), channel_id=1, source_target_pairs={{0,7},{1,0},{2,1},{3,2},{4,3},{5,4},{6,5},{7,6},{8,15},{9,8},{10,9... | collective-permute-start | bytes 98312 | tf_op jit(solution)/shard_map/while/body/eval_jaxpr/ppermute | solution.py:79
  108.4 6.6 %collective-permute-start.5 = (f32[1,64,128]{2,1,0:T(8,128)S(1)}, f32[1,64,128]{2,1,0:T(8,128)S(1)}, u32[]{:S(2)}, u32[]{:S(2)}) collective-permute-start(f32[1,64,128]{2,1,0:T(8,128)S(1)} %collective-permute-done.4), channel_id=1, source_target_pairs={{0,1},{1,2},{2,3},{3,4},{4,5},{5,6},{6,7},{7,0},{8,9},{9,10},{10,1... | collective-permute-start | bytes 98312 | tf_op jit(solution)/shard_map/while/body/eval_jaxpr/ppermute | solution.py:77
  120.3 6.6 %collective-permute-start.2 = (f32[1,64,128]{2,1,0:T(8,128)S(1)}, f32[1,64,128]{2,1,0:T(8,128)S(1)}, u32[]{:S(2)}, u32[]{:S(2)}) collective-permute-start(f32[1,64,128]{2,1,0:T(8,128)S(1)} %bitcast.91), channel_id=1, source_target_pairs={{0,1},{1,2},{2,3},{3,4},{4,5},{5,6},{6,7},{7,0},{8,9},{9,10},{10,1... | collective-permute-start | bytes 98312 | tf_op jit(solution)/shard_map/while/body/eval_jaxpr/ppermute | solution.py:77
  120.3 6.6 %collective-permute-start.6 = (f32[1,64,128]{2,1,0:T(8,128)S(1)}, f32[1,64,128]{2,1,0:T(8,128)S(1)}, u32[]{:S(2)}, u32[]{:S(2)}) collective-permute-start(f32[1,64,128]{2,1,0:T(8,128)S(1)} %bitcast.92), channel_id=1, source_target_pairs={{0,7},{1,0},{2,1},{3,2},{4,3},{5,4},{6,5},{7,6},{8,15},{9,8},{10,9... | collective-permute-start | bytes 98312 | tf_op jit(solution)/shard_map/while/body/eval_jaxpr/ppermute | solution.py:79
  126.9 6.6 %collective-permute-start.3 = (f32[1,64,128]{2,1,0:T(8,128)S(1)}, f32[1,64,128]{2,1,0:T(8,128)S(1)}, u32[]{:S(2)}, u32[]{:S(2)}) collective-permute-start(f32[1,64,128]{2,1,0:T(8,128)S(1)} %collective-permute-done.2), channel_id=1, source_target_pairs={{0,1},{1,2},{2,3},{3,4},{4,5},{5,6},{6,7},{7,0},{8,9},{9,10},{10,1... | collective-permute-start | bytes 98312 | tf_op jit(solution)/shard_map/while/body/eval_jaxpr/ppermute | solution.py:77
  126.9 6.6 %collective-permute-start.7 = (f32[1,64,128]{2,1,0:T(8,128)S(1)}, f32[1,64,128]{2,1,0:T(8,128)S(1)}, u32[]{:S(2)}, u32[]{:S(2)}) collective-permute-start(f32[1,64,128]{2,1,0:T(8,128)S(1)} %collective-permute-done.6), channel_id=1, source_target_pairs={{0,7},{1,0},{2,1},{3,2},{4,3},{5,4},{6,5},{7,6},{8,15},{9,8},{10,9... | collective-permute-start | bytes 98312 | tf_op jit(solution)/shard_map/while/body/eval_jaxpr/ppermute | solution.py:79
  133.5 6.6 %collective-permute-start.4 = (f32[1,64,128]{2,1,0:T(8,128)S(1)}, f32[1,64,128]{2,1,0:T(8,128)S(1)}, u32[]{:S(2)}, u32[]{:S(2)}) collective-permute-start(f32[1,64,128]{2,1,0:T(8,128)S(1)} %collective-permute-done.3), channel_id=1, source_target_pairs={{0,1},{1,2},{2,3},{3,4},{4,5},{5,6},{6,7},{7,0},{8,9},{9,10},{10,1... | collective-permute-start | bytes 98312 | tf_op jit(solution)/shard_map/while/body/eval_jaxpr/ppermute | solution.py:77
  133.5 6.6 %collective-permute-start.8 = (f32[1,64,128]{2,1,0:T(8,128)S(1)}, f32[1,64,128]{2,1,0:T(8,128)S(1)}, u32[]{:S(2)}, u32[]{:S(2)}) collective-permute-start(f32[1,64,128]{2,1,0:T(8,128)S(1)} %collective-permute-done.7), channel_id=1, source_target_pairs={{0,7},{1,0},{2,1},{3,2},{4,3},{5,4},{6,5},{7,6},{8,15},{9,8},{10,9... | collective-permute-start | bytes 98312 | tf_op jit(solution)/shard_map/while/body/eval_jaxpr/ppermute | solution.py:79
  140.1 6.6 %collective-permute-start.5 = (f32[1,64,128]{2,1,0:T(8,128)S(1)}, f32[1,64,128]{2,1,0:T(8,128)S(1)}, u32[]{:S(2)}, u32[]{:S(2)}) collective-permute-start(f32[1,64,128]{2,1,0:T(8,128)S(1)} %collective-permute-done.4), channel_id=1, source_target_pairs={{0,1},{1,2},{2,3},{3,4},{4,5},{5,6},{6,7},{7,0},{8,9},{9,10},{10,1... | collective-permute-start | bytes 98312 | tf_op jit(solution)/shard_map/while/body/eval_jaxpr/ppermute | solution.py:77
  152.0 6.6 %collective-permute-start.2 = (f32[1,64,128]{2,1,0:T(8,128)S(1)}, f32[1,64,128]{2,1,0:T(8,128)S(1)}, u32[]{:S(2)}, u32[]{:S(2)}) collective-permute-start(f32[1,64,128]{2,1,0:T(8,128)S(1)} %bitcast.91), channel_id=1, source_target_pairs={{0,1},{1,2},{2,3},{3,4},{4,5},{5,6},{6,7},{7,0},{8,9},{9,10},{10,1... | collective-permute-start | bytes 98312 | tf_op jit(solution)/shard_map/while/body/eval_jaxpr/ppermute | solution.py:77
  152.0 6.6 %collective-permute-start.6 = (f32[1,64,128]{2,1,0:T(8,128)S(1)}, f32[1,64,128]{2,1,0:T(8,128)S(1)}, u32[]{:S(2)}, u32[]{:S(2)}) collective-permute-start(f32[1,64,128]{2,1,0:T(8,128)S(1)} %bitcast.92), channel_id=1, source_target_pairs={{0,7},{1,0},{2,1},{3,2},{4,3},{5,4},{6,5},{7,6},{8,15},{9,8},{10,9... | collective-permute-start | bytes 98312 | tf_op jit(solution)/shard_map/while/body/eval_jaxpr/ppermute | solution.py:79
  158.6 6.6 %collective-permute-start.3 = (f32[1,64,128]{2,1,0:T(8,128)S(1)}, f32[1,64,128]{2,1,0:T(8,128)S(1)}, u32[]{:S(2)}, u32[]{:S(2)}) collective-permute-start(f32[1,64,128]{2,1,0:T(8,128)S(1)} %collective-permute-done.2), channel_id=1, source_target_pairs={{0,1},{1,2},{2,3},{3,4},{4,5},{5,6},{6,7},{7,0},{8,9},{9,10},{10,1... | collective-permute-start | bytes 98312 | tf_op jit(solution)/shard_map/while/body/eval_jaxpr/ppermute | solution.py:77
  158.6 6.6 %collective-permute-start.7 = (f32[1,64,128]{2,1,0:T(8,128)S(1)}, f32[1,64,128]{2,1,0:T(8,128)S(1)}, u32[]{:S(2)}, u32[]{:S(2)}) collective-permute-start(f32[1,64,128]{2,1,0:T(8,128)S(1)} %collective-permute-done.6), channel_id=1, source_target_pairs={{0,7},{1,0},{2,1},{3,2},{4,3},{5,4},{6,5},{7,6},{8,15},{9,8},{10,9... | collective-permute-start | bytes 98312 | tf_op jit(solution)/shard_map/while/body/eval_jaxpr/ppermute | solution.py:79
  165.2 6.6 %collective-permute-start.4 = (f32[1,64,128]{2,1,0:T(8,128)S(1)}, f32[1,64,128]{2,1,0:T(8,128)S(1)}, u32[]{:S(2)}, u32[]{:S(2)}) collective-permute-start(f32[1,64,128]{2,1,0:T(8,128)S(1)} %collective-permute-done.3), channel_id=1, source_target_pairs={{0,1},{1,2},{2,3},{3,4},{4,5},{5,6},{6,7},{7,0},{8,9},{9,10},{10,1... | collective-permute-start | bytes 98312 | tf_op jit(solution)/shard_map/while/body/eval_jaxpr/ppermute | solution.py:77
  165.3 6.6 %collective-permute-start.8 = (f32[1,64,128]{2,1,0:T(8,128)S(1)}, f32[1,64,128]{2,1,0:T(8,128)S(1)}, u32[]{:S(2)}, u32[]{:S(2)}) collective-permute-start(f32[1,64,128]{2,1,0:T(8,128)S(1)} %collective-permute-done.7), channel_id=1, source_target_pairs={{0,7},{1,0},{2,1},{3,2},{4,3},{5,4},{6,5},{7,6},{8,15},{9,8},{10,9... | collective-permute-start | bytes 98312 | tf_op jit(solution)/shard_map/while/body/eval_jaxpr/ppermute | solution.py:79
  171.9 6.6 %collective-permute-start.5 = (f32[1,64,128]{2,1,0:T(8,128)S(1)}, f32[1,64,128]{2,1,0:T(8,128)S(1)}, u32[]{:S(2)}, u32[]{:S(2)}) collective-permute-start(f32[1,64,128]{2,1,0:T(8,128)S(1)} %collective-permute-done.4), channel_id=1, source_target_pairs={{0,1},{1,2},{2,3},{3,4},{4,5},{5,6},{6,7},{7,0},{8,9},{9,10},{10,1... | collective-permute-start | bytes 98312 | tf_op jit(solution)/shard_map/while/body/eval_jaxpr/ppermute | solution.py:77
  183.8 6.6 %collective-permute-start.2 = (f32[1,64,128]{2,1,0:T(8,128)S(1)}, f32[1,64,128]{2,1,0:T(8,128)S(1)}, u32[]{:S(2)}, u32[]{:S(2)}) collective-permute-start(f32[1,64,128]{2,1,0:T(8,128)S(1)} %bitcast.91), channel_id=1, source_target_pairs={{0,1},{1,2},{2,3},{3,4},{4,5},{5,6},{6,7},{7,0},{8,9},{9,10},{10,1... | collective-permute-start | bytes 98312 | tf_op jit(solution)/shard_map/while/body/eval_jaxpr/ppermute | solution.py:77
  183.8 6.6 %collective-permute-start.6 = (f32[1,64,128]{2,1,0:T(8,128)S(1)}, f32[1,64,128]{2,1,0:T(8,128)S(1)}, u32[]{:S(2)}, u32[]{:S(2)}) collective-permute-start(f32[1,64,128]{2,1,0:T(8,128)S(1)} %bitcast.92), channel_id=1, source_target_pairs={{0,7},{1,0},{2,1},{3,2},{4,3},{5,4},{6,5},{7,6},{8,15},{9,8},{10,9... | collective-permute-start | bytes 98312 | tf_op jit(solution)/shard_map/while/body/eval_jaxpr/ppermute | solution.py:79
  190.4 6.6 %collective-permute-start.3 = (f32[1,64,128]{2,1,0:T(8,128)S(1)}, f32[1,64,128]{2,1,0:T(8,128)S(1)}, u32[]{:S(2)}, u32[]{:S(2)}) collective-permute-start(f32[1,64,128]{2,1,0:T(8,128)S(1)} %collective-permute-done.2), channel_id=1, source_target_pairs={{0,1},{1,2},{2,3},{3,4},{4,5},{5,6},{6,7},{7,0},{8,9},{9,10},{10,1... | collective-permute-start | bytes 98312 | tf_op jit(solution)/shard_map/while/body/eval_jaxpr/ppermute | solution.py:77
  190.4 6.6 %collective-permute-start.7 = (f32[1,64,128]{2,1,0:T(8,128)S(1)}, f32[1,64,128]{2,1,0:T(8,128)S(1)}, u32[]{:S(2)}, u32[]{:S(2)}) collective-permute-start(f32[1,64,128]{2,1,0:T(8,128)S(1)} %collective-permute-done.6), channel_id=1, source_target_pairs={{0,7},{1,0},{2,1},{3,2},{4,3},{5,4},{6,5},{7,6},{8,15},{9,8},{10,9... | collective-permute-start | bytes 98312 | tf_op jit(solution)/shard_map/while/body/eval_jaxpr/ppermute | solution.py:79
  197.0 6.6 %collective-permute-start.4 = (f32[1,64,128]{2,1,0:T(8,128)S(1)}, f32[1,64,128]{2,1,0:T(8,128)S(1)}, u32[]{:S(2)}, u32[]{:S(2)}) collective-permute-start(f32[1,64,128]{2,1,0:T(8,128)S(1)} %collective-permute-done.3), channel_id=1, source_target_pairs={{0,1},{1,2},{2,3},{3,4},{4,5},{5,6},{6,7},{7,0},{8,9},{9,10},{10,1... | collective-permute-start | bytes 98312 | tf_op jit(solution)/shard_map/while/body/eval_jaxpr/ppermute | solution.py:77
  197.0 6.6 %collective-permute-start.8 = (f32[1,64,128]{2,1,0:T(8,128)S(1)}, f32[1,64,128]{2,1,0:T(8,128)S(1)}, u32[]{:S(2)}, u32[]{:S(2)}) collective-permute-start(f32[1,64,128]{2,1,0:T(8,128)S(1)} %collective-permute-done.7), channel_id=1, source_target_pairs={{0,7},{1,0},{2,1},{3,2},{4,3},{5,4},{6,5},{7,6},{8,15},{9,8},{10,9... | collective-permute-start | bytes 98312 | tf_op jit(solution)/shard_map/while/body/eval_jaxpr/ppermute | solution.py:79
  203.6 6.6 %collective-permute-start.5 = (f32[1,64,128]{2,1,0:T(8,128)S(1)}, f32[1,64,128]{2,1,0:T(8,128)S(1)}, u32[]{:S(2)}, u32[]{:S(2)}) collective-permute-start(f32[1,64,128]{2,1,0:T(8,128)S(1)} %collective-permute-done.4), channel_id=1, source_target_pairs={{0,1},{1,2},{2,3},{3,4},{4,5},{5,6},{6,7},{7,0},{8,9},{9,10},{10,1... | collective-permute-start | bytes 98312 | tf_op jit(solution)/shard_map/while/body/eval_jaxpr/ppermute | solution.py:77
  (11 other events, 140.2 us)
